TPU v7x, 512 devices: a whole 4x8x8 slice. The times are simulated.
512 devices in a mesh: axial: 64 (over x, z, core), radial: 8 (over y).
Axes of the slice: x: 4, y: 8, z: 8, core: 2. Of those that a mesh axis runs over, the one named last changes fastest.
Arguments:
- state_start: float32 [5, 640, 128, 128], P(None, 'axial', 'radial'), may hold values from -6 to 6
- forcing: float32 [640, 128, 128], P('axial', 'radial'), may hold values from -6 to 6
- signal: float32 [8], replicated, may hold values from -1 to 1
- mixing: float32 [2, 5, 5], replicated, may hold values from -0.4 to 0.4
- panel_cell: int32 [64, 8, 64, 4], P('axial', 'radial'), may hold values from -1 to 20479, as said below
- amplitude: float32 [64, 8, 64, 4, 512], P('axial', 'radial'), may hold values from -0.015625 to 0.015625
- delay: float32 [64, 8, 64, 4, 512], P('axial', 'radial'), may hold values from 0 to 8
- observer_list: int32 [512], replicated, may hold values from 0 to 511, each once
Outputs:
- final_state: float32 [5, 640, 128, 128], P(None, 'axial', 'radial')
- spectra: float32 [2, 4, 512], P(None, None, ('axial', 'radial'))
- adjoint_state: float32 [5, 640, 128, 128], P(None, 'axial', 'radial')
- forcing_grad: float32 [640, 128, 128], P('axial', 'radial')
Inputs may be any that keep to these rules, and one draw needn't show every extreme that they name: `panel_cell`: each entry is a cell index of the sending tile, of 20480 cells, or -1 for an empty slot; the live slots of one tile and owner come first; one owner in each draw receives 4 live slots from every tile, and the largest cell index is reached.
All inputs are finite; a program needn't handle non-finite values.
Results may differ from a plain program's by a relative error of at most 0.0003.
Values sent between devices are 32-bit elements; how exact they have to be, the bound alone decides.
A program may use at most 128 MiB of HBM per device.

v0:
```python
import math
import jax
import jax.numpy as jnp
from jax import lax
from jax.sharding import PartitionSpec as P

STEPS = 8
FREQ = 4
deriv_coef = (5.0 / 6.0, -5.0 / 21.0, 5.0 / 84.0, -5.0 / 504.0, 1.0 / 1260.0)
filter_coef = tuple(
    ((-1.0) ** abs(offset) * math.comb(10, 5 + offset) / 1024.0 for offset in range(-5, 6))
)
damping = 0.2
highest = lax.Precision.HIGHEST


def extended(block, sides, width):
    for axis, dim in sides:
        count = lax.axis_size(axis)
        forward = [(i, i + 1) for i in range(count - 1)]
        backward = [(target, source) for source, target in forward]
        low = lax.ppermute(
            lax.slice_in_dim(block, block.shape[dim] - width, None, axis=dim), axis, forward
        )
        high = lax.ppermute(lax.slice_in_dim(block, 0, width, axis=dim), axis, backward)
        block = jnp.concatenate([low, block, high], axis=dim)
    return block


def advance(padded, mixing, adjoint):
    span_x = padded.shape[1] - 10
    span_r = padded.shape[2] - 10
    count = padded.shape[0]

    def along_x(offset):
        return padded[:, 5 + offset : 5 + offset + span_x, 5 : 5 + span_r, :]

    def along_r(offset):
        return padded[:, 5 : 5 + span_x, 5 + offset : 5 + offset + span_r, :]

    centre = along_x(0)
    deriv_x = sum(
        (deriv_coef[order] * (along_x(order + 1) - along_x(-order - 1)) for order in range(5))
    )
    deriv_r = sum(
        (deriv_coef[order] * (along_r(order + 1) - along_r(-order - 1)) for order in range(5))
    )
    smooth = sum(
        (filter_coef[offset + 5] * (along_x(offset) + along_r(offset)) for offset in range(-5, 6))
    )
    factor = 1.0 if adjoint else -1.0
    outputs = []
    for target in range(count):
        term = centre[target] - damping * smooth[target]
        for source in range(count):
            if adjoint:
                coef_x = mixing[0, source, target]
                coef_r = mixing[1, source, target]
            else:
                coef_x = mixing[0, target, source]
                coef_r = mixing[1, target, source]
            term = term + factor * (coef_x * deriv_x[source] + coef_r * deriv_r[source])
        outputs.append(term)
    return jnp.stack(outputs)


def frequencies():
    return 2.0 * jnp.pi * (jnp.arange(FREQ, dtype=jnp.float32) + 1.0) / STEPS


def time_tables():
    levels = jnp.arange(STEPS, dtype=jnp.float32)
    phase = levels[:, None] * frequencies()[None, :]
    return (jnp.cos(phase), jnp.sin(phase))


def panel_kernels(amp, lag):
    phase = frequencies()[None, :, None] * lag[:, None, :]
    return (amp[:, None, :] * jnp.cos(phase), -amp[:, None, :] * jnp.sin(phase))


def partial_spectra(panels, kern_re, kern_im, cos_t, sin_t):
    coef_re = jnp.dot(panels, cos_t, precision=highest)
    coef_im = -jnp.dot(panels, sin_t, precision=highest)
    spec_re = jnp.einsum("pfo,pf->fo", kern_re, coef_re, precision=highest) - jnp.einsum(
        "pfo,pf->fo", kern_im, coef_im, precision=highest
    )
    spec_im = jnp.einsum("pfo,pf->fo", kern_re, coef_im, precision=highest) + jnp.einsum(
        "pfo,pf->fo", kern_im, coef_re, precision=highest
    )
    return jnp.stack([spec_re, spec_im])


def panel_sources(spectra, kern_re, kern_im, cos_t, sin_t):
    back_re = jnp.einsum("pfo,fo->pf", kern_re, spectra[0], precision=highest) + jnp.einsum(
        "pfo,fo->pf", kern_im, spectra[1], precision=highest
    )
    back_im = jnp.einsum("pfo,fo->pf", kern_im, spectra[0], precision=highest) - jnp.einsum(
        "pfo,fo->pf", kern_re, spectra[1], precision=highest
    )
    return 2.0 * (
        jnp.dot(back_re, cos_t.T, precision=highest) + jnp.dot(back_im, sin_t.T, precision=highest)
    )


def on_device(state_start, forcing, signal, mixing, panel_cell, amplitude, delay, observer_list):
    slots = panel_cell[0, 0]
    cell_total = forcing.shape[0] * forcing.shape[1] * forcing.shape[2]
    live = slots >= 0
    targets = jnp.where(live, slots, cell_total)
    clipped = jnp.minimum(targets, cell_total - 1)
    state = state_start
    records = []
    for level in range(STEPS):
        padded = extended(state, (("axial", 1), ("radial", 2)), 5)
        state = advance(padded, mixing, False).at[4].add(signal[level] * forcing)
        records.append(jnp.where(live, jnp.take(state[4].reshape(-1), clipped), 0.0))
    stacked = jnp.stack(records, axis=-1)
    received = lax.all_to_all(stacked, "axial", split_axis=0, concat_axis=0, tiled=True)
    observers = observer_list.shape[0]
    chosen_amp = jnp.take(amplitude[0, 0], observer_list, axis=2).reshape(-1, observers)
    chosen_lag = jnp.take(delay[0, 0], observer_list, axis=2).reshape(-1, observers)
    kern_re, kern_im = panel_kernels(chosen_amp, chosen_lag)
    cos_t, sin_t = time_tables()
    partial_sum = partial_spectra(received.reshape(-1, STEPS), kern_re, kern_im, cos_t, sin_t)
    share = observers // lax.axis_size(("axial", "radial"))
    total = lax.psum(partial_sum, ("axial", "radial"))
    mine = lax.dynamic_slice_in_dim(total, lax.axis_index(("axial", "radial")) * share, share, 2)
    sources = panel_sources(total, kern_re, kern_im, cos_t, sin_t).reshape(received.shape)
    returned = lax.all_to_all(sources, "axial", split_axis=0, concat_axis=0, tiled=True)
    flat_targets = targets.reshape(-1)
    adjoint = jnp.zeros_like(state_start)
    gradient = jnp.zeros_like(forcing)
    for level in reversed(range(STEPS)):
        spread = (
            jnp.zeros((cell_total,), jnp.float32)
            .at[flat_targets]
            .add(returned[:, :, level].reshape(-1), mode="drop")
        )
        carried = adjoint.at[4].add(spread.reshape(forcing.shape))
        gradient = gradient + signal[level] * carried[4]
        padded = extended(carried, (("axial", 1), ("radial", 2)), 5)
        adjoint = advance(padded, mixing, True)
    return (state, mine, adjoint, gradient)


def solution(mesh):
    return jax.shard_map(
        on_device,
        mesh=mesh,
        in_specs=(
            P(None, "axial", "radial", None),
            P("axial", "radial", None),
            P(),
            P(),
            P("axial", "radial", None, None),
            P("axial", "radial", None, None, None),
            P("axial", "radial", None, None, None),
            P(),
        ),
        out_specs=(
            P(None, "axial", "radial", None),
            P(None, None, ("axial", "radial")),
            P(None, "axial", "radial", None),
            P("axial", "radial", None),
        ),
        check_vma=False,
    )
```

profile of v0, /device:TPU:64, one launch (start us, length us, event | category | flops | bytes accessed | tf_op | source)
XLA Modules:
  0.0 1145.9 jit_solution(15424200699040122054)
XLA Ops:
  19.7 7.2 collective-permute-done.3
  29.7 6.4 constant_dynamic-update-slice_fusion.11
  36.1 6.3 constant_dynamic-update-slice_fusion.10
  42.4 6.4 constant_dynamic-update-slice_fusion.9
  48.9 6.3 constant_dynamic-update-slice_fusion.8
  77.0 7.1 collective-permute-done.6
  90.4 6.4 constant_dynamic-update-slice_fusion.16
  96.7 6.3 constant_dynamic-update-slice_fusion.15
  103.1 6.5 constant_dynamic-update-slice_fusion.14
  109.5 6.3 constant_dynamic-update-slice_fusion.13
  148.3 6.4 constant_dynamic-update-slice_fusion.21
  154.7 6.3 constant_dynamic-update-slice_fusion.20
  161.0 6.4 constant_dynamic-update-slice_fusion.19
  167.5 6.3 constant_dynamic-update-slice_fusion.18
  214.7 6.4 constant_dynamic-update-slice_fusion.26
  221.1 6.3 constant_dynamic-update-slice_fusion.25
  227.4 6.4 constant_dynamic-update-slice_fusion.24
  233.9 6.3 constant_dynamic-update-slice_fusion.23
  240.2 6.3 constant_dynamic-update-slice_fusion.22
  281.9 6.4 constant_dynamic-update-slice_fusion.31
  288.3 6.3 constant_dynamic-update-slice_fusion.30
  294.6 6.4 constant_dynamic-update-slice_fusion.29
  340.7 6.4 constant_dynamic-update-slice_fusion.36
  347.1 6.3 constant_dynamic-update-slice_fusion.35
  353.4 6.4 constant_dynamic-update-slice_fusion.34
  359.9 6.3 constant_dynamic-update-slice_fusion.33
  401.3 6.4 constant_dynamic-update-slice_fusion.41
  407.7 6.3 constant_dynamic-update-slice_fusion.40
  414.0 6.4 constant_dynamic-update-slice_fusion.39
  460.8 6.4 constant_dynamic-update-slice_fusion.46
  467.2 6.3 constant_dynamic-update-slice_fusion.45
  473.5 6.4 constant_dynamic-update-slice_fusion.44
  498.4 18.4 %all-to-all-start = ((f32[64,4,8]{2,1,0:T(4,128)}), f32[64,4,8]{2,1,0:T(4,128)S(1)}, u32[]{:S(2)}, u32[]{:S(2)}) async-start(f32[64,4,8]{2,1,0:T(4,128)} %copy.48), calls=%async_computation | async-start | bytes 262144 | tf_op jit(solution)/shard_map/all_to_all | solution.py:119
  516.8 17.0 %fusion = (f32[256,4,512]{2,1,0:T(4,128)}, f32[256,4,512]{2,1,0:T(4,128)}) fusion(f32[256,512]{1,0:T(8,128)S(1)} %mul.7300, f32[4]{0:T(128)S(1)} %add_multiply_fusion, f32[256,512]{1,0:T(8,128)S(1)} %mul.7297, f32[256,512]{1,0:T(8,128)S(1)} %neg.11), kind=kLoop, calls=%fused_computation.28 | loop fusion | flops 1572864 | bytes 5767184 | tf_op jit(solution)/shard_map/mul | solution.py:79
  546.9 96.8 %psum.7 = f32[2,4,512]{2,1,0:T(4,128)S(1)} all-reduce(f32[2,4,512]{2,1,0:T(4,128)S(1)} %pad_maximum_fusion.62), channel_id=1, replica_groups=mesh['axial'=64,'radial'=8] {'axial','radial'}, use_global_device_ids=true, to_apply=%region_0.3 | all-reduce | flops 4096 | bytes 32768 | tf_op jit(solution)/shard_map/psum | solution.py:127
  651.4 7.6 all-to-all-start.1
  659.1 10.0 all-to-all-done.1
  685.1 8.0 collective-permute-done.34
  705.0 6.3 constant_dynamic-update-slice_fusion.58
  711.3 6.5 constant_dynamic-update-slice_fusion.57
  717.8 6.4 constant_dynamic-update-slice_fusion.56
  764.4 6.3 constant_dynamic-update-slice_fusion.63
  770.7 6.5 constant_dynamic-update-slice_fusion.62
  777.2 6.4 constant_dynamic-update-slice_fusion.61
  823.5 6.3 constant_dynamic-update-slice_fusion.68
  829.8 6.5 constant_dynamic-update-slice_fusion.67
  836.3 6.4 constant_dynamic-update-slice_fusion.66
  881.6 6.3 constant_dynamic-update-slice_fusion.73
  887.9 6.5 constant_dynamic-update-slice_fusion.72
  894.4 6.4 constant_dynamic-update-slice_fusion.71
  939.3 6.3 constant_dynamic-update-slice_fusion.78
  945.6 6.5 constant_dynamic-update-slice_fusion.77
  952.2 6.4 constant_dynamic-update-slice_fusion.76
  997.0 6.3 constant_dynamic-update-slice_fusion.83
  1003.3 6.5 constant_dynamic-update-slice_fusion.82
  1009.8 6.4 constant_dynamic-update-slice_fusion.81
  1055.7 6.3 constant_dynamic-update-slice_fusion.88
  1062.0 6.5 constant_dynamic-update-slice_fusion.87
  1068.5 6.4 constant_dynamic-update-slice_fusion.86
  1074.9 11.2 bitcast_add_fusion
  1100.5 7.3 collective-permute-done.62
  1119.6 6.3 constant_dynamic-update-slice_fusion.93
  1125.9 6.5 constant_dynamic-update-slice_fusion.92
  1132.4 6.4 constant_dynamic-update-slice_fusion.91
  (392 shorter events, 607.6 us)
Async XLA Ops:
  1.8 10.9 collective-permute-start
  3.7 9.1 collective-permute-start.1
  12.9 14.0 %collective-permute-start.3 = (f32[5,20,5,128]{3,2,1,0:T(8,128)S(1)}, f32[5,20,5,128]{3,2,1,0:T(8,128)S(1)}, u32[]{:S(2)}, u32[]{:S(2)}) collective-permute-start(f32[5,20,5,128]{3,2,1,0:T(8,128)S(1)} %get-tuple-element.337), channel_id=1, source_target_pairs={{1,0},{2,1},{3,2},{4,3},{5,4},{6,5},{7,6},{9,8},{10,9},{11,10},{12... | collective-permute-start | bytes 768008 | tf_op jit(solution)/shard_map/ppermute | solution.py:25
  14.2 13.9 %collective-permute-start.2 = (f32[5,20,5,128]{3,2,1,0:T(8,128)S(1)}, f32[5,20,5,128]{3,2,1,0:T(8,128)S(1)}, u32[]{:S(2)}, u32[]{:S(2)}) collective-permute-start(f32[5,20,5,128]{3,2,1,0:T(8,128)S(1)} %get-tuple-element.338), channel_id=1, source_target_pairs={{0,1},{1,2},{2,3},{3,4},{4,5},{5,6},{6,7},{8,9},{9,10},{10,11},{11... | collective-permute-start | bytes 768008 | tf_op jit(solution)/shard_map/ppermute | solution.py:22
  62.1 7.4 collective-permute-start.4
  64.0 7.2 collective-permute-start.5
  71.3 12.8 %collective-permute-start.6 = (f32[5,20,5,128]{3,2,1,0:T(8,128)S(1)}, f32[5,20,5,128]{3,2,1,0:T(8,128)S(1)}, u32[]{:S(2)}, u32[]{:S(2)}) collective-permute-start(f32[5,20,5,128]{3,2,1,0:T(8,128)S(1)} %get-tuple-element.335), channel_id=1, source_target_pairs={{0,1},{1,2},{2,3},{3,4},{4,5},{5,6},{6,7},{8,9},{9,10},{10,11},{11... | collective-permute-start | bytes 768008 | tf_op jit(solution)/shard_map/ppermute | solution.py:22
  75.7 13.1 %collective-permute-start.7 = (f32[5,20,5,128]{3,2,1,0:T(8,128)S(1)}, f32[5,20,5,128]{3,2,1,0:T(8,128)S(1)}, u32[]{:S(2)}, u32[]{:S(2)}) collective-permute-start(f32[5,20,5,128]{3,2,1,0:T(8,128)S(1)} %get-tuple-element.336), channel_id=1, source_target_pairs={{1,0},{2,1},{3,2},{4,3},{5,4},{6,5},{7,6},{9,8},{10,9},{11,10},{12... | collective-permute-start | bytes 768008 | tf_op jit(solution)/shard_map/ppermute | solution.py:25
  122.8 7.1 collective-permute-start.8
  131.7 9.5 collective-permute-start.10
  134.4 12.6 %collective-permute-start.11 = (f32[5,20,5,128]{3,2,1,0:T(8,128)S(1)}, f32[5,20,5,128]{3,2,1,0:T(8,128)S(1)}, u32[]{:S(2)}, u32[]{:S(2)}) collective-permute-start(f32[5,20,5,128]{3,2,1,0:T(8,128)S(1)} %get-tuple-element.332), channel_id=1, source_target_pairs={{1,0},{2,1},{3,2},{4,3},{5,4},{6,5},{7,6},{9,8},{10,9},{11,10},{12... | collective-permute-start | bytes 768008 | tf_op jit(solution)/shard_map/ppermute | solution.py:25
  181.5 14.0 %collective-permute-start.12 = (f32[5,5,16,128]{3,2,1,0:T(8,128)}, f32[5,5,16,128]{3,2,1,0:T(8,128)S(1)}, u32[]{:S(2)}, u32[]{:S(2)}) collective-permute-start(f32[5,5,16,128]{3,2,1,0:T(8,128)} %get-tuple-element.363), channel_id=1, source_target_pairs={{0,8},{8,16},{16,24},{24,32},{32,40},{40,48},{48,56},{56,64},{64,7... | collective-permute-start | bytes 614408 | tf_op jit(solution)/shard_map/ppermute | solution.py:22
  186.2 9.2 collective-permute-start.13
  195.6 12.9 %collective-permute-start.14 = (f32[5,20,5,128]{3,2,1,0:T(8,128)S(1)}, f32[5,20,5,128]{3,2,1,0:T(8,128)S(1)}, u32[]{:S(2)}, u32[]{:S(2)}) collective-permute-start(f32[5,20,5,128]{3,2,1,0:T(8,128)S(1)} %get-tuple-element.327), channel_id=1, source_target_pairs={{0,1},{1,2},{2,3},{3,4},{4,5},{5,6},{6,7},{8,9},{9,10},{10,11},{11... | collective-permute-start | bytes 768008 | tf_op jit(solution)/shard_map/ppermute | solution.py:22
  201.0 12.4 %collective-permute-start.15 = (f32[5,20,5,128]{3,2,1,0:T(8,128)S(1)}, f32[5,20,5,128]{3,2,1,0:T(8,128)S(1)}, u32[]{:S(2)}, u32[]{:S(2)}) collective-permute-start(f32[5,20,5,128]{3,2,1,0:T(8,128)S(1)} %get-tuple-element.328), channel_id=1, source_target_pairs={{1,0},{2,1},{3,2},{4,3},{5,4},{6,5},{7,6},{9,8},{10,9},{11,10},{12... | collective-permute-start | bytes 768008 | tf_op jit(solution)/shard_map/ppermute | solution.py:25
  247.9 12.4 %collective-permute-start.16 = (f32[5,5,16,128]{3,2,1,0:T(8,128)}, f32[5,5,16,128]{3,2,1,0:T(8,128)S(1)}, u32[]{:S(2)}, u32[]{:S(2)}) collective-permute-start(f32[5,5,16,128]{3,2,1,0:T(8,128)} %get-tuple-element.361), channel_id=1, source_target_pairs={{0,8},{8,16},{16,24},{24,32},{32,40},{40,48},{48,56},{56,64},{64,7... | collective-permute-start | bytes 614408 | tf_op jit(solution)/shard_map/ppermute | solution.py:22
  251.7 8.6 collective-permute-start.17
  261.2 12.9 %collective-permute-start.18 = (f32[5,20,5,128]{3,2,1,0:T(8,128)}, f32[5,20,5,128]{3,2,1,0:T(8,128)}, u32[]{:S(2)}, u32[]{:S(2)}) collective-permute-start(f32[5,20,5,128]{3,2,1,0:T(8,128)} %get-tuple-element.323), channel_id=1, source_target_pairs={{0,1},{1,2},{2,3},{3,4},{4,5},{5,6},{6,7},{8,9},{9,10},{10,11},{11... | collective-permute-start | bytes 768008 | tf_op jit(solution)/shard_map/ppermute | solution.py:22
  266.1 13.4 %collective-permute-start.19 = (f32[5,20,5,128]{3,2,1,0:T(8,128)S(1)}, f32[5,20,5,128]{3,2,1,0:T(8,128)}, u32[]{:S(2)}, u32[]{:S(2)}) collective-permute-start(f32[5,20,5,128]{3,2,1,0:T(8,128)S(1)} %get-tuple-element.324), channel_id=1, source_target_pairs={{1,0},{2,1},{3,2},{4,3},{5,4},{6,5},{7,6},{9,8},{10,9},{11,10},{12... | collective-permute-start | bytes 768008 | tf_op jit(solution)/shard_map/ppermute | solution.py:25
  314.1 8.0 collective-permute-start.20
  316.8 6.1 collective-permute-start.21
  323.8 9.2 collective-permute-start.22
  326.3 12.0 %collective-permute-start.23 = (f32[5,20,5,128]{3,2,1,0:T(8,128)S(1)}, f32[5,20,5,128]{3,2,1,0:T(8,128)}, u32[]{:S(2)}, u32[]{:S(2)}) collective-permute-start(f32[5,20,5,128]{3,2,1,0:T(8,128)S(1)} %get-tuple-element.320), channel_id=1, source_target_pairs={{1,0},{2,1},{3,2},{4,3},{5,4},{6,5},{7,6},{9,8},{10,9},{11,10},{12... | collective-permute-start | bytes 768008 | tf_op jit(solution)/shard_map/ppermute | solution.py:25
  373.0 8.5 collective-permute-start.24
  383.6 9.8 collective-permute-start.26
  387.4 11.5 %collective-permute-start.27 = (f32[5,20,5,128]{3,2,1,0:T(8,128)S(1)}, f32[5,20,5,128]{3,2,1,0:T(8,128)}, u32[]{:S(2)}, u32[]{:S(2)}) collective-permute-start(f32[5,20,5,128]{3,2,1,0:T(8,128)S(1)} %get-tuple-element.316), channel_id=1, source_target_pairs={{1,0},{2,1},{3,2},{4,3},{5,4},{6,5},{7,6},{9,8},{10,9},{11,10},{12... | collective-permute-start | bytes 768008 | tf_op jit(solution)/shard_map/ppermute | solution.py:25
  433.6 9.2 collective-permute-start.28
  438.4 7.0 collective-permute-start.29
  445.5 9.3 collective-permute-start.30
  448.3 11.2 collective-permute-start.31
  498.4 40.4 %all-to-all-start = ((f32[64,4,8]{2,1,0:T(4,128)}), f32[64,4,8]{2,1,0:T(4,128)S(1)}, u32[]{:S(2)}, u32[]{:S(2)}) async-start(f32[64,4,8]{2,1,0:T(4,128)} %copy.48), calls=%async_computation | async-start | bytes 262144 | tf_op jit(solution)/shard_map/all_to_all | solution.py:119
  651.4 17.7 %all-to-all-start.1 = ((f32[64,4,8]{2,1,0:T(4,128)}), f32[64,4,8]{2,1,0:T(4,128)S(1)}, u32[]{:S(2)}, u32[]{:S(2)}) async-start(f32[64,4,8]{2,1,0:T(4,128)} %bitcast.105), calls=%async_computation.1 | async-start | bytes 262144 | tf_op jit(solution)/shard_map/all_to_all | solution.py:130
  672.3 7.7 collective-permute-start.32
  674.3 6.8 collective-permute-start.33
  681.3 11.8 %collective-permute-start.34 = (f32[5,20,5,128]{3,2,1,0:T(8,128)S(1)}, f32[5,20,5,128]{3,2,1,0:T(8,128)S(1)}, u32[]{:S(2)}, u32[]{:S(2)}) collective-permute-start(f32[5,20,5,128]{3,2,1,0:T(8,128)S(1)} %get-tuple-element.307), channel_id=1, source_target_pairs={{0,1},{1,2},{2,3},{3,4},{4,5},{5,6},{6,7},{8,9},{9,10},{10,11},{11... | collective-permute-start | bytes 768008 | tf_op jit(solution)/shard_map/ppermute | solution.py:22
  683.4 14.0 %collective-permute-start.35 = (f32[5,20,5,128]{3,2,1,0:T(8,128)S(1)}, f32[5,20,5,128]{3,2,1,0:T(8,128)S(1)}, u32[]{:S(2)}, u32[]{:S(2)}) collective-permute-start(f32[5,20,5,128]{3,2,1,0:T(8,128)S(1)} %get-tuple-element.308), channel_id=1, source_target_pairs={{1,0},{2,1},{3,2},{4,3},{5,4},{6,5},{7,6},{9,8},{10,9},{11,10},{12... | collective-permute-start | bytes 768008 | tf_op jit(solution)/shard_map/ppermute | solution.py:25
  730.4 7.1 collective-permute-start.36
  732.3 6.9 collective-permute-start.37
  739.3 13.0 %collective-permute-start.38 = (f32[5,20,5,128]{3,2,1,0:T(8,128)S(1)}, f32[5,20,5,128]{3,2,1,0:T(8,128)S(1)}, u32[]{:S(2)}, u32[]{:S(2)}) collective-permute-start(f32[5,20,5,128]{3,2,1,0:T(8,128)S(1)} %get-tuple-element.303), channel_id=1, source_target_pairs={{0,1},{1,2},{2,3},{3,4},{4,5},{5,6},{6,7},{8,9},{9,10},{10,11},{11... | collective-permute-start | bytes 768008 | tf_op jit(solution)/shard_map/ppermute | solution.py:22
  742.6 14.2 %collective-permute-start.39 = (f32[5,20,5,128]{3,2,1,0:T(8,128)S(1)}, f32[5,20,5,128]{3,2,1,0:T(8,128)S(1)}, u32[]{:S(2)}, u32[]{:S(2)}) collective-permute-start(f32[5,20,5,128]{3,2,1,0:T(8,128)S(1)} %get-tuple-element.304), channel_id=1, source_target_pairs={{1,0},{2,1},{3,2},{4,3},{5,4},{6,5},{7,6},{9,8},{10,9},{11,10},{12... | collective-permute-start | bytes 768008 | tf_op jit(solution)/shard_map/ppermute | solution.py:25
  789.8 7.1 collective-permute-start.40
  791.8 6.8 collective-permute-start.41
  798.8 13.1 %collective-permute-start.42 = (f32[5,20,5,128]{3,2,1,0:T(8,128)S(1)}, f32[5,20,5,128]{3,2,1,0:T(8,128)S(1)}, u32[]{:S(2)}, u32[]{:S(2)}) collective-permute-start(f32[5,20,5,128]{3,2,1,0:T(8,128)S(1)} %get-tuple-element.299), channel_id=1, source_target_pairs={{0,1},{1,2},{2,3},{3,4},{4,5},{5,6},{6,7},{8,9},{9,10},{10,11},{11... | collective-permute-start | bytes 768008 | tf_op jit(solution)/shard_map/ppermute | solution.py:22
  802.5 13.4 %collective-permute-start.43 = (f32[5,20,5,128]{3,2,1,0:T(8,128)S(1)}, f32[5,20,5,128]{3,2,1,0:T(8,128)S(1)}, u32[]{:S(2)}, u32[]{:S(2)}) collective-permute-start(f32[5,20,5,128]{3,2,1,0:T(8,128)S(1)} %get-tuple-element.300), channel_id=1, source_target_pairs={{1,0},{2,1},{3,2},{4,3},{5,4},{6,5},{7,6},{9,8},{10,9},{11,10},{12... | collective-permute-start | bytes 768008 | tf_op jit(solution)/shard_map/ppermute | solution.py:25
  848.9 7.1 collective-permute-start.44
  850.9 6.9 collective-permute-start.45
  857.9 12.0 %collective-permute-start.46 = (f32[5,20,5,128]{3,2,1,0:T(8,128)S(1)}, f32[5,20,5,128]{3,2,1,0:T(8,128)S(1)}, u32[]{:S(2)}, u32[]{:S(2)}) collective-permute-start(f32[5,20,5,128]{3,2,1,0:T(8,128)S(1)} %get-tuple-element.295), channel_id=1, source_target_pairs={{0,1},{1,2},{2,3},{3,4},{4,5},{5,6},{6,7},{8,9},{9,10},{10,11},{11... | collective-permute-start | bytes 768008 | tf_op jit(solution)/shard_map/ppermute | solution.py:22
  861.6 12.5 %collective-permute-start.47 = (f32[5,20,5,128]{3,2,1,0:T(8,128)S(1)}, f32[5,20,5,128]{3,2,1,0:T(8,128)S(1)}, u32[]{:S(2)}, u32[]{:S(2)}) collective-permute-start(f32[5,20,5,128]{3,2,1,0:T(8,128)S(1)} %get-tuple-element.296), channel_id=1, source_target_pairs={{1,0},{2,1},{3,2},{4,3},{5,4},{6,5},{7,6},{9,8},{10,9},{11,10},{12... | collective-permute-start | bytes 768008 | tf_op jit(solution)/shard_map/ppermute | solution.py:25
  907.0 7.1 collective-permute-start.48
  909.0 6.9 collective-permute-start.49
  916.0 11.6 %collective-permute-start.50 = (f32[5,20,5,128]{3,2,1,0:T(8,128)S(1)}, f32[5,20,5,128]{3,2,1,0:T(8,128)S(1)}, u32[]{:S(2)}, u32[]{:S(2)}) collective-permute-start(f32[5,20,5,128]{3,2,1,0:T(8,128)S(1)} %get-tuple-element.291), channel_id=1, source_target_pairs={{0,1},{1,2},{2,3},{3,4},{4,5},{5,6},{6,7},{8,9},{9,10},{10,11},{11... | collective-permute-start | bytes 768008 | tf_op jit(solution)/shard_map/ppermute | solution.py:22
  919.5 12.3 %collective-permute-start.51 = (f32[5,20,5,128]{3,2,1,0:T(8,128)S(1)}, f32[5,20,5,128]{3,2,1,0:T(8,128)S(1)}, u32[]{:S(2)}, u32[]{:S(2)}) collective-permute-start(f32[5,20,5,128]{3,2,1,0:T(8,128)S(1)} %get-tuple-element.292), channel_id=1, source_target_pairs={{1,0},{2,1},{3,2},{4,3},{5,4},{6,5},{7,6},{9,8},{10,9},{11,10},{12... | collective-permute-start | bytes 768008 | tf_op jit(solution)/shard_map/ppermute | solution.py:25
  964.7 7.1 collective-permute-start.52
  966.7 6.9 collective-permute-start.53
  973.7 11.6 %collective-permute-start.54 = (f32[5,20,5,128]{3,2,1,0:T(8,128)S(1)}, f32[5,20,5,128]{3,2,1,0:T(8,128)S(1)}, u32[]{:S(2)}, u32[]{:S(2)}) collective-permute-start(f32[5,20,5,128]{3,2,1,0:T(8,128)S(1)} %get-tuple-element.287), channel_id=1, source_target_pairs={{0,1},{1,2},{2,3},{3,4},{4,5},{5,6},{6,7},{8,9},{9,10},{10,11},{11... | collective-permute-start | bytes 768008 | tf_op jit(solution)/shard_map/ppermute | solution.py:22
  976.9 12.5 %collective-permute-start.55 = (f32[5,20,5,128]{3,2,1,0:T(8,128)S(1)}, f32[5,20,5,128]{3,2,1,0:T(8,128)S(1)}, u32[]{:S(2)}, u32[]{:S(2)}) collective-permute-start(f32[5,20,5,128]{3,2,1,0:T(8,128)S(1)} %get-tuple-element.288), channel_id=1, source_target_pairs={{1,0},{2,1},{3,2},{4,3},{5,4},{6,5},{7,6},{9,8},{10,9},{11,10},{12... | collective-permute-start | bytes 768008 | tf_op jit(solution)/shard_map/ppermute | solution.py:25
  1022.4 7.1 collective-permute-start.56
  1024.3 6.9 collective-permute-start.57
  1031.4 12.6 %collective-permute-start.58 = (f32[5,20,5,128]{3,2,1,0:T(8,128)S(1)}, f32[5,20,5,128]{3,2,1,0:T(8,128)S(1)}, u32[]{:S(2)}, u32[]{:S(2)}) collective-permute-start(f32[5,20,5,128]{3,2,1,0:T(8,128)S(1)} %get-tuple-element.283), channel_id=1, source_target_pairs={{0,1},{1,2},{2,3},{3,4},{4,5},{5,6},{6,7},{8,9},{9,10},{10,11},{11... | collective-permute-start | bytes 768008 | tf_op jit(solution)/shard_map/ppermute | solution.py:22
  1034.6 13.5 %collective-permute-start.59 = (f32[5,20,5,128]{3,2,1,0:T(8,128)S(1)}, f32[5,20,5,128]{3,2,1,0:T(8,128)S(1)}, u32[]{:S(2)}, u32[]{:S(2)}) collective-permute-start(f32[5,20,5,128]{3,2,1,0:T(8,128)S(1)} %get-tuple-element.284), channel_id=1, source_target_pairs={{1,0},{2,1},{3,2},{4,3},{5,4},{6,5},{7,6},{9,8},{10,9},{11,10},{12... | collective-permute-start | bytes 768008 | tf_op jit(solution)/shard_map/ppermute | solution.py:25
  1086.1 7.1 collective-permute-start.60
  1088.0 6.9 collective-permute-start.61
  1095.1 12.8 %collective-permute-start.62 = (f32[5,20,5,128]{3,2,1,0:T(8,128)S(1)}, f32[5,20,5,128]{3,2,1,0:T(8,128)S(1)}, u32[]{:S(2)}, u32[]{:S(2)}) collective-permute-start(f32[5,20,5,128]{3,2,1,0:T(8,128)S(1)} %get-tuple-element.279), channel_id=1, source_target_pairs={{0,1},{1,2},{2,3},{3,4},{4,5},{5,6},{6,7},{8,9},{9,10},{10,11},{11... | collective-permute-start | bytes 768008 | tf_op jit(solution)/shard_map/ppermute | solution.py:22
  1098.3 13.7 %collective-permute-start.63 = (f32[5,20,5,128]{3,2,1,0:T(8,128)S(1)}, f32[5,20,5,128]{3,2,1,0:T(8,128)S(1)}, u32[]{:S(2)}, u32[]{:S(2)}) collective-permute-start(f32[5,20,5,128]{3,2,1,0:T(8,128)S(1)} %get-tuple-element.280), channel_id=1, source_target_pairs={{1,0},{2,1},{3,2},{4,3},{5,4},{6,5},{7,6},{9,8},{10,9},{11,10},{12... | collective-permute-start | bytes 768008 | tf_op jit(solution)/shard_map/ppermute | solution.py:25
  (14 other events, 115.5 us)
where the time goes:
time: 1160 us; the launch traced here: 1150 us
  other arithmetic  585 us (50%)
  waiting for transfers between devices  200 us (17%)
  starting transfers between devices  196 us (17%)
  blocking collectives  96.8 us (8%)
  local copies, waits for them, and re-layouts  49.8 us (4%)
  matrix products  14.5 us (1%)
    unnamed x71, other arithmetic  411 us
    ppermute x32, starting transfers between devices, extended(): lax.ppermute(lax.slice_in_dim(block, block.shape[dim] - width, None, axis...  99.1 us
    ppermute x32, waiting for transfers between devices, extended(): lax.ppermute(lax.slice_in_dim(block, 0, width, axis=dim), axis, backward)  98.5 us
    psum x1, blocking collectives, on_device(): total = lax.psum(partial_sum, ('axial', 'radial'))  96.8 us
    another operation x15, other arithmetic, advance(): return jnp.stack(outputs)  92.6 us
    ppermute x32, waiting for transfers between devices, extended(): lax.ppermute(lax.slice_in_dim(block, block.shape[dim] - width, None, axis...  91.8 us
    ppermute x32, starting transfers between devices, extended(): lax.ppermute(lax.slice_in_dim(block, 0, width, axis=dim), axis, backward)  71 us
  transfers between devices with their start and end apart: 66, of which 55 were waited for; matrix products, arithmetic and copies ran while one was open for 7% of the time, Pallas kernels for 0%

commit v1 on v0

--- a/solution.py
+++ b/solution.py
@@ -12,6 +12,11 @@
 )
 damping = 0.2
 highest = lax.Precision.HIGHEST
+
+
+def read_tails(u, named_axis):
+    g_now = jnp.sum(jax.lax.all_gather(u, axis_name=named_axis), 0)
+    return g_now
 
 
 def extended(block, sides, width):
@@ -124,7 +129,7 @@
     cos_t, sin_t = time_tables()
     partial_sum = partial_spectra(received.reshape(-1, STEPS), kern_re, kern_im, cos_t, sin_t)
     share = observers // lax.axis_size(("axial", "radial"))
-    total = lax.psum(partial_sum, ("axial", "radial"))
+    total = read_tails(partial_sum, named_axis=("axial", "radial"))
     mine = lax.dynamic_slice_in_dim(total, lax.axis_index(("axial", "radial")) * share, share, 2)
     sources = panel_sources(total, kern_re, kern_im, cos_t, sin_t).reshape(received.shape)
     returned = lax.all_to_all(sources, "axial", split_axis=0, concat_axis=0, tiled=True)

time: 1160 us -> 1210 us (1.043)
  the two profiles are of different devices: /device:TPU:64 before, /device:TPU:2 now
where the time goes in v1:
time: 1210 us; the launch traced here: 1190 us
  other arithmetic  586 us (48%)
  waiting for transfers between devices  286 us (24%)
  starting transfers between devices  237 us (20%)
  local copies, waits for them, and re-layouts  49.9 us (4%)
  between operations  16.6 us (1%)
  matrix products  14.5 us (1%)
    unnamed x71, other arithmetic  403 us
    ppermute x32, starting transfers between devices, extended(): lax.ppermute(lax.slice_in_dim(block, 0, width, axis=dim), axis, backward)  125 us
    all_gather x1, waiting for transfers between devices, read_tails(): g_now = jnp.sum(jax.lax.all_gather(u, axis_name=named_axis), 0)  124 us
    another operation x15, other arithmetic, advance(): return jnp.stack(outputs)  95.9 us
    ppermute x32, starting transfers between devices, extended(): lax.ppermute(lax.slice_in_dim(block, block.shape[dim] - width, None, axis...  91.2 us
    ppermute x32, waiting for transfers between devices, extended(): lax.ppermute(lax.slice_in_dim(block, 0, width, axis=dim), axis, backward)  90 us
    ppermute x32, waiting for transfers between devices, extended(): lax.ppermute(lax.slice_in_dim(block, block.shape[dim] - width, None, axis...  62.6 us
  transfers between devices with their start and end apart: 67, of which 56 were waited for; matrix products, arithmetic and copies ran while one was open for 6% of the time, Pallas kernels for 0%

profile of v1, /device:TPU:2, one launch (start us, length us, event | category | flops | bytes accessed | tf_op | source)
XLA Modules:
  0.0 1189.7 jit_solution(3566010077796977237)
XLA Ops:
  10.2 10.4 collective-permute-start.1
  39.1 6.3 constant_dynamic-update-slice_fusion.11
  45.3 6.3 constant_dynamic-update-slice_fusion.10
  51.6 6.2 constant_dynamic-update-slice_fusion.9
  64.1 6.4 constant_dynamic-update-slice_fusion.7
  99.2 6.3 constant_dynamic-update-slice_fusion.16
  105.5 6.3 constant_dynamic-update-slice_fusion.15
  111.8 6.2 constant_dynamic-update-slice_fusion.14
  124.2 6.4 constant_dynamic-update-slice_fusion.12
  133.2 8.0 collective-permute-start.9
  160.6 6.3 constant_dynamic-update-slice_fusion.21
  166.9 6.3 constant_dynamic-update-slice_fusion.20
  173.2 6.2 constant_dynamic-update-slice_fusion.19
  185.6 6.4 constant_dynamic-update-slice_fusion.17
  195.3 7.7 collective-permute-start.13
  227.5 6.3 constant_dynamic-update-slice_fusion.26
  233.8 6.3 constant_dynamic-update-slice_fusion.25
  240.1 6.2 constant_dynamic-update-slice_fusion.24
  252.5 6.5 constant_dynamic-update-slice_fusion.22
  292.9 6.3 constant_dynamic-update-slice_fusion.31
  299.1 6.3 constant_dynamic-update-slice_fusion.30
  305.4 6.2 constant_dynamic-update-slice_fusion.29
  317.8 6.4 constant_dynamic-update-slice_fusion.27
  352.3 6.3 constant_dynamic-update-slice_fusion.36
  358.6 6.3 constant_dynamic-update-slice_fusion.35
  364.9 6.2 constant_dynamic-update-slice_fusion.34
  377.3 6.4 constant_dynamic-update-slice_fusion.32
  386.3 7.9 collective-permute-start.25
  414.1 6.3 constant_dynamic-update-slice_fusion.41
  420.3 6.3 constant_dynamic-update-slice_fusion.40
  426.6 6.2 constant_dynamic-update-slice_fusion.39
  439.0 6.4 constant_dynamic-update-slice_fusion.37
  448.0 7.1 collective-permute-start.29
  472.5 6.3 constant_dynamic-update-slice_fusion.46
  478.8 6.3 constant_dynamic-update-slice_fusion.45
  485.1 6.2 constant_dynamic-update-slice_fusion.44
  497.5 6.4 constant_dynamic-update-slice_fusion.42
  509.8 12.0 %all-to-all-start = ((f32[64,4,8]{2,1,0:T(4,128)}), f32[64,4,8]{2,1,0:T(4,128)S(1)}, u32[]{:S(2)}, u32[]{:S(2)}) async-start(f32[64,4,8]{2,1,0:T(4,128)} %copy.64), calls=%async_computation | async-start | bytes 262144 | tf_op jit(solution)/shard_map/all_to_all | solution.py:124
  521.9 17.0 %fusion = (f32[256,4,512]{2,1,0:T(4,128)}, f32[256,4,512]{2,1,0:T(4,128)}) fusion(f32[256,512]{1,0:T(8,128)S(1)} %mul.7300, f32[4]{0:T(128)S(1)} %add_multiply_fusion, f32[256,512]{1,0:T(8,128)S(1)} %mul.7297, f32[256,512]{1,0:T(8,128)S(1)} %neg.11), kind=kLoop, calls=%fused_computation.28 | loop fusion | flops 1572864 | bytes 5767184 | tf_op jit(solution)/shard_map/mul | solution.py:84
  552.9 123.6 %all-gather.3.cloned.1.call-done = f32[1024,4,512]{2,1,0:T(4,128)} async-done(((f32[2,4,512]{2,1,0:T(4,128)}), f32[1024,4,512]{2,1,0:T(4,128)}) %all-gather.3.cloned.1.call-update) | async-done | bytes 8388624 | tf_op jit(solution)/shard_map/all_gather | solution.py:18
  688.7 8.7 all-to-all-start.1
  697.4 9.4 all-to-all-done.1
  725.7 6.8 collective-permute-done.34
  738.0 6.3 constant_dynamic-update-slice_fusion.59
  762.9 6.4 constant_dynamic-update-slice_fusion.55
  796.8 6.3 constant_dynamic-update-slice_fusion.64
  809.3 6.2 constant_dynamic-update-slice_fusion.62
  821.7 6.4 constant_dynamic-update-slice_fusion.60
  856.8 6.3 constant_dynamic-update-slice_fusion.69
  869.3 6.2 constant_dynamic-update-slice_fusion.67
  881.7 6.4 constant_dynamic-update-slice_fusion.65
  915.6 6.3 constant_dynamic-update-slice_fusion.74
  928.2 6.2 constant_dynamic-update-slice_fusion.72
  940.6 6.4 constant_dynamic-update-slice_fusion.70
  973.8 6.3 constant_dynamic-update-slice_fusion.79
  986.3 6.2 constant_dynamic-update-slice_fusion.77
  998.7 6.4 constant_dynamic-update-slice_fusion.75
  1031.1 6.3 constant_dynamic-update-slice_fusion.84
  1043.6 6.2 constant_dynamic-update-slice_fusion.82
  1056.0 6.4 constant_dynamic-update-slice_fusion.80
  1088.4 6.3 constant_dynamic-update-slice_fusion.89
  1113.3 11.5 bitcast_add_fusion
  1150.6 6.3 constant_dynamic-update-slice_fusion.94
  1175.5 6.4 constant_dynamic-update-slice_fusion.90
  (395 shorter events, 615.3 us)
Async XLA Ops:
  8.3 17.6 %collective-permute-start = (f32[5,5,16,128]{3,2,1,0:T(8,128)S(1)}, f32[5,5,16,128]{3,2,1,0:T(8,128)S(1)}, u32[]{:S(2)}, u32[]{:S(2)}) collective-permute-start(f32[5,5,16,128]{3,2,1,0:T(8,128)S(1)} %get-tuple-element.372), channel_id=1, source_target_pairs={{0,8},{8,16},{16,24},{24,32},{32,40},{40,48},{48,56},{56,64},{64,7... | collective-permute-start | bytes 614408 | tf_op jit(solution)/shard_map/ppermute | solution.py:27
  10.2 15.8 %collective-permute-start.1 = (f32[5,5,16,128]{3,2,1,0:T(8,128)S(1)}, f32[5,5,16,128]{3,2,1,0:T(8,128)S(1)}, u32[]{:S(2)}, u32[]{:S(2)}) collective-permute-start(f32[5,5,16,128]{3,2,1,0:T(8,128)S(1)} %get-tuple-element.373), channel_id=1, source_target_pairs={{8,0},{16,8},{24,16},{32,24},{40,32},{48,40},{56,48},{64,56},{72,6... | collective-permute-start | bytes 614408 | tf_op jit(solution)/shard_map/ppermute | solution.py:30
  26.2 9.8 collective-permute-start.3
  27.5 10.0 collective-permute-start.2
  71.2 9.2 collective-permute-start.4
  73.1 9.0 collective-permute-start.5
  82.3 11.3 collective-permute-start.6
  86.7 11.0 collective-permute-start.7
  131.3 11.4 collective-permute-start.8
  133.2 11.2 collective-permute-start.9
  144.6 8.9 collective-permute-start.10
  148.1 11.2 collective-permute-start.11
  193.4 16.9 %collective-permute-start.12 = (f32[5,5,16,128]{3,2,1,0:T(8,128)}, f32[5,5,16,128]{3,2,1,0:T(8,128)S(1)}, u32[]{:S(2)}, u32[]{:S(2)}) collective-permute-start(f32[5,5,16,128]{3,2,1,0:T(8,128)} %get-tuple-element.363), channel_id=1, source_target_pairs={{0,8},{8,16},{16,24},{24,32},{32,40},{40,48},{48,56},{56,64},{64,7... | collective-permute-start | bytes 614408 | tf_op jit(solution)/shard_map/ppermute | solution.py:27
  195.3 15.0 %collective-permute-start.13 = (f32[5,5,16,128]{3,2,1,0:T(8,128)}, f32[5,5,16,128]{3,2,1,0:T(8,128)S(1)}, u32[]{:S(2)}, u32[]{:S(2)}) collective-permute-start(f32[5,5,16,128]{3,2,1,0:T(8,128)} %get-tuple-element.364), channel_id=1, source_target_pairs={{8,0},{16,8},{24,16},{32,24},{40,32},{48,40},{56,48},{64,56},{72,6... | collective-permute-start | bytes 614408 | tf_op jit(solution)/shard_map/ppermute | solution.py:30
  210.5 10.8 collective-permute-start.14
  216.3 9.8 collective-permute-start.15
  260.5 14.4 %collective-permute-start.16 = (f32[5,5,16,128]{3,2,1,0:T(8,128)}, f32[5,5,16,128]{3,2,1,0:T(8,128)S(1)}, u32[]{:S(2)}, u32[]{:S(2)}) collective-permute-start(f32[5,5,16,128]{3,2,1,0:T(8,128)} %get-tuple-element.361), channel_id=1, source_target_pairs={{0,8},{8,16},{16,24},{24,32},{32,40},{40,48},{48,56},{56,64},{64,7... | collective-permute-start | bytes 614408 | tf_op jit(solution)/shard_map/ppermute | solution.py:27
  262.4 12.5 %collective-permute-start.17 = (f32[5,5,16,128]{3,2,1,0:T(8,128)}, f32[5,5,16,128]{3,2,1,0:T(8,128)S(1)}, u32[]{:S(2)}, u32[]{:S(2)}) collective-permute-start(f32[5,5,16,128]{3,2,1,0:T(8,128)} %get-tuple-element.362), channel_id=1, source_target_pairs={{8,0},{16,8},{24,16},{32,24},{40,32},{48,40},{56,48},{64,56},{72,6... | collective-permute-start | bytes 614408 | tf_op jit(solution)/shard_map/ppermute | solution.py:30
  275.8 9.7 collective-permute-start.18
  280.4 9.9 collective-permute-start.19
  325.0 10.1 collective-permute-start.20
  326.9 9.0 collective-permute-start.21
  339.9 9.9 collective-permute-start.23
  384.4 12.3 %collective-permute-start.24 = (f32[5,5,16,128]{3,2,1,0:T(8,128)S(1)}, f32[5,5,16,128]{3,2,1,0:T(8,128)S(1)}, u32[]{:S(2)}, u32[]{:S(2)}) collective-permute-start(f32[5,5,16,128]{3,2,1,0:T(8,128)S(1)} %get-tuple-element.357), channel_id=1, source_target_pairs={{0,8},{8,16},{16,24},{24,32},{32,40},{40,48},{48,56},{56,64},{64,7... | collective-permute-start | bytes 614408 | tf_op jit(solution)/shard_map/ppermute | solution.py:27
  386.3 11.2 collective-permute-start.25
  401.6 9.9 collective-permute-start.27
  446.1 11.5 collective-permute-start.28
  448.0 10.3 collective-permute-start.29
  461.4 9.8 collective-permute-start.31
  509.8 34.1 %all-to-all-start = ((f32[64,4,8]{2,1,0:T(4,128)}), f32[64,4,8]{2,1,0:T(4,128)S(1)}, u32[]{:S(2)}, u32[]{:S(2)}) async-start(f32[64,4,8]{2,1,0:T(4,128)} %copy.64), calls=%async_computation | async-start | bytes 262144 | tf_op jit(solution)/shard_map/all_to_all | solution.py:124
  521.9 154.6 %all-gather.3.cloned.1.call-start = ((), (), s32[]{:S(2)}) async-start(), calls=%async_computation.2 | async-start | bytes 8404992 | tf_op jit(solution)/shard_map/all_gather | solution.py:18
  688.7 18.1 %all-to-all-start.1 = ((f32[64,4,8]{2,1,0:T(4,128)}), f32[64,4,8]{2,1,0:T(4,128)S(1)}, u32[]{:S(2)}, u32[]{:S(2)}) async-start(f32[64,4,8]{2,1,0:T(4,128)} %bitcast.106), calls=%async_computation.1 | async-start | bytes 262144 | tf_op jit(solution)/shard_map/all_to_all | solution.py:135
  710.0 9.8 collective-permute-start.32
  712.0 8.9 collective-permute-start.33
  721.1 11.5 collective-permute-start.34
  724.2 12.5 %collective-permute-start.35 = (f32[5,20,5,128]{3,2,1,0:T(8,128)S(1)}, f32[5,20,5,128]{3,2,1,0:T(8,128)S(1)}, u32[]{:S(2)}, u32[]{:S(2)}) collective-permute-start(f32[5,20,5,128]{3,2,1,0:T(8,128)S(1)} %get-tuple-element.308), channel_id=1, source_target_pairs={{1,0},{2,1},{3,2},{4,3},{5,4},{6,5},{7,6},{9,8},{10,9},{11,10},{12... | collective-permute-start | bytes 768008 | tf_op jit(solution)/shard_map/ppermute | solution.py:30
  769.4 9.2 collective-permute-start.36
  771.3 9.0 collective-permute-start.37
  780.5 10.8 collective-permute-start.38
  783.5 11.9 %collective-permute-start.39 = (f32[5,20,5,128]{3,2,1,0:T(8,128)S(1)}, f32[5,20,5,128]{3,2,1,0:T(8,128)S(1)}, u32[]{:S(2)}, u32[]{:S(2)}) collective-permute-start(f32[5,20,5,128]{3,2,1,0:T(8,128)S(1)} %get-tuple-element.304), channel_id=1, source_target_pairs={{1,0},{2,1},{3,2},{4,3},{5,4},{6,5},{7,6},{9,8},{10,9},{11,10},{12... | collective-permute-start | bytes 768008 | tf_op jit(solution)/shard_map/ppermute | solution.py:30
  828.2 9.2 collective-permute-start.40
  830.1 9.0 collective-permute-start.41
  839.2 11.9 %collective-permute-start.42 = (f32[5,20,5,128]{3,2,1,0:T(8,128)S(1)}, f32[5,20,5,128]{3,2,1,0:T(8,128)S(1)}, u32[]{:S(2)}, u32[]{:S(2)}) collective-permute-start(f32[5,20,5,128]{3,2,1,0:T(8,128)S(1)} %get-tuple-element.299), channel_id=1, source_target_pairs={{0,1},{1,2},{2,3},{3,4},{4,5},{5,6},{6,7},{8,9},{9,10},{10,11},{11... | collective-permute-start | bytes 768008 | tf_op jit(solution)/shard_map/ppermute | solution.py:27
  843.6 11.9 collective-permute-start.43
  888.2 9.2 collective-permute-start.44
  890.1 9.0 collective-permute-start.45
  899.3 10.9 collective-permute-start.46
  902.9 11.3 collective-permute-start.47
  947.0 9.2 collective-permute-start.48
  948.9 9.0 collective-permute-start.49
  958.1 10.2 collective-permute-start.50
  961.5 11.0 collective-permute-start.51
  1005.2 9.2 collective-permute-start.52
  1007.1 9.0 collective-permute-start.53
  1016.3 9.4 collective-permute-start.54
  1019.8 9.9 collective-permute-start.55
  1062.5 9.2 collective-permute-start.56
  1064.4 9.0 collective-permute-start.57
  1073.6 9.1 collective-permute-start.58
  1077.2 9.8 collective-permute-start.59
  1124.9 9.2 collective-permute-start.60
  1126.8 9.0 collective-permute-start.61
  1136.0 9.0 collective-permute-start.62
  1139.4 9.8 collective-permute-start.63
  (15 other events, 150.6 us)
Sparse Core Ops, SparseCore 0:
  552.9 123.5 all-gather.2
